TPU v7x, 512 devices: a whole 4x8x8 slice. The times are simulated.
512 devices in a mesh: geo: 128 (over y, z, core), deg: 4 (over x).
Axes of the slice: x: 4, y: 8, z: 8, core: 2. Of those that a mesh axis runs over, the one named last changes fastest.
Arguments:
- lo_ainv: bfloat16 [20, 20, 65536], P(None, None, ('geo', 'deg')), may hold values from -1.25 to 1.25
- lo_geom: float32 [12, 65536], P(None, ('geo', 'deg')), may hold values from -1.5 to 1.5
- lo_load: bfloat16 [20, 65536], P(None, ('geo', 'deg')), may hold values from -6 to 6
- lo_degree: int32 [65536], P(('geo', 'deg')), may hold values from 1 to 3, as said below
- lo_send: int32 [4, 65536], P(None, ('geo', 'deg')), may hold values from 0 to 767, as said below
- hi_geom: float32 [12, 65536], P(None, ('geo', 'deg')), may hold values from -1.5 to 1.5
- hi_load: bfloat16 [84, 65536], P(None, ('geo', 'deg')), may hold values from -6 to 6
- hi_degree: int32 [65536], P(('geo', 'deg')), may hold values from 0 to 6, as said below
- hi_slot: int32 [65536], P(('geo', 'deg')), may hold values from -1 to 127, as said below
- hi_ainv: bfloat16 [84, 84, 65536], P(None, None, ('geo', 'deg')), may hold values from -0.625 to 0.625
- hi_send: int32 [4, 65536], P(None, ('geo', 'deg')), may hold values from -1 to 767, as said below
- recv_face: int32 [786432], P(('geo', 'deg')), may hold values from -1 to 767, as said below
- lift_ref: float32 [4, 4, 28, 84], replicated, may hold values from -1.25 to 1.25
- trace_ref: float32 [4, 84, 4, 28], replicated, may hold values from -1.25 to 1.25
- face_mass: float32 [28, 28], replicated, may hold values from -2 to 2
Outputs:
- low_particular: float32 [20, 65536], P(None, ('geo', 'deg'))
- high_particular: float32 [84, 65536], P(None, ('geo', 'deg'))
- trace_blocks: float32 [28, 28, 393216], P(None, None, ('geo', 'deg'))
- trace_rhs: float32 [28, 393216], P(None, ('geo', 'deg'))
Inputs may be any that keep to these rules, and one draw needn't show every extreme that they name: `lo_degree`: every LOW position holds an element of degree 1, 2 or 3. `hi_degree`: 0 where the position holds no element, else 4, 5 or 6. `hi_slot`: -1 exactly where hi_degree is 0; the other values are distinct on a device, so at most 32 elements go from one device to one device of its deg group; in some geo index every batch slot is filled. `lo_send`: values are distinct on a device, so at most 6 rows go from one device to one owner; some owners receive 6 LOW rows from every device of their deg index. `hi_send`: -1 exactly for the faces of batch slots that receive no element; the other values are distinct on a device; some owners receive 6 HIGH rows from every device of their deg index. `recv_face`: -1 exactly where no row arrives; a face of a device is named at most twice among that device's entries.
All inputs are finite; a program needn't handle non-finite values.
Results may differ from a plain program's by a relative error of at most 0.0095.
Values may be sent and summed in bfloat16 or wider, within the bound.
A program may use at most 64 MiB of HBM per device.

v0:
```python
import jax
import jax.numpy as jnp
from jax import lax
from jax.sharding import PartitionSpec as P

NI_LO = 20
NF_LO = 10


def prefix_masks(degree_value, inner_width, face_width):
    inner_count = (degree_value + 1.0) * (degree_value + 2.0) * (degree_value + 3.0) / 6.0
    face_count = (degree_value + 1.0) * (degree_value + 2.0) / 2.0
    inner_mask = (
        jnp.arange(inner_width, dtype=jnp.float32)[:, None] < inner_count[None, :]
    ).astype(jnp.float32)
    face_mask = (jnp.arange(face_width, dtype=jnp.float32)[:, None] < face_count[None, :]).astype(
        jnp.float32
    )
    return (inner_mask, face_mask)


def condense(inverse, geometry, load_values, degree_value, lift_table, trace_table, mass_table):
    term_count = lift_table.shape[0]
    face_width = mass_table.shape[0]
    element_count = geometry.shape[1]
    inner_mask, face_mask = prefix_masks(degree_value, inverse.shape[0], face_width)
    lift_mix = jnp.einsum(
        "kaij,ke->aije", lift_table, geometry[:term_count], precision=lax.Precision.HIGHEST
    )
    lift_mat = (lift_mix * face_mask[None, :, None, :] * inner_mask[None, None, :, :]).astype(
        jnp.bfloat16
    )
    trace_mix = jnp.einsum(
        "kjai,ke->jaie",
        trace_table,
        geometry[term_count : 2 * term_count],
        precision=lax.Precision.HIGHEST,
    )
    trace_mat = (trace_mix * inner_mask[:, None, None, :] * face_mask[None, None, :, :]).astype(
        jnp.bfloat16
    )
    solved = jnp.einsum(
        "jle,laie->jaie", inverse, trace_mat, preferred_element_type=jnp.float32
    ).astype(jnp.bfloat16)
    coupling = jnp.einsum("aije,jame->imae", lift_mat, solved, preferred_element_type=jnp.float32)
    scaling = geometry[2 * term_count : 2 * term_count + 4]
    pair_mask = face_mask[:, None, :] * face_mask[None, :, :]
    schur_block = (
        mass_table[:, :, None, None] * scaling[None, None, :, :] * pair_mask[:, :, None, :]
        - coupling
    )
    masked_load = load_values * inner_mask.astype(jnp.bfloat16)
    particular = inner_mask * jnp.einsum(
        "jle,le->je", inverse, masked_load, preferred_element_type=jnp.float32
    )
    rhs_part = -jnp.einsum(
        "aije,je->iae",
        lift_mat,
        particular.astype(jnp.bfloat16),
        preferred_element_type=jnp.float32,
    )
    face_rows = jnp.concatenate(
        [
            schur_block.reshape(face_width * face_width, 4 * element_count),
            rhs_part.reshape(face_width, 4 * element_count),
        ],
        axis=0,
    )
    return (face_rows.astype(jnp.bfloat16), particular)


def fill_buffer(face_rows, positions, slot_total):
    target = jnp.where(positions < 0, slot_total, positions)
    empty_buffer = jnp.zeros((face_rows.shape[0], slot_total), face_rows.dtype)
    return empty_buffer.at[:, target].set(face_rows, mode="drop")


def embed_rows(face_rows, narrow, wide_face):
    row_count = face_rows.shape[1]
    block_part = face_rows[: narrow * narrow].reshape(narrow, narrow, row_count)
    block_part = jnp.pad(block_part, ((0, wide_face - narrow), (0, wide_face - narrow), (0, 0)))
    right_part = jnp.pad(face_rows[narrow * narrow :], ((0, wide_face - narrow), (0, 0)))
    return jnp.concatenate(
        [block_part.reshape(wide_face * wide_face, row_count), right_part], axis=0
    )


def accumulate(blocks, right_side, arrived_rows, receive_plan, narrow):
    face_total = blocks.shape[2]
    block_width = min(512, face_total)
    pieces = []
    begin = 0
    while begin < face_total:
        width_here = min(block_width, face_total - begin)
        columns = begin + jnp.arange(width_here, dtype=jnp.int32)
        selector = (receive_plan[:, None] == columns[None, :]).astype(jnp.bfloat16)
        pieces.append(jnp.dot(arrived_rows, selector, preferred_element_type=jnp.float32))
        begin = begin + width_here
    summed = jnp.concatenate(pieces, axis=1)
    block_part = summed[: narrow * narrow].reshape(narrow, narrow, face_total)
    blocks = blocks.at[:narrow, :narrow].add(block_part)
    right_side = right_side.at[:narrow].add(summed[narrow * narrow :])
    return (blocks, right_side)


def on_device(
    lo_ainv,
    lo_geom,
    lo_load,
    lo_degree,
    lo_send,
    hi_geom,
    hi_load,
    hi_degree,
    hi_slot,
    hi_ainv,
    hi_send,
    recv_face,
    lift_ref,
    trace_ref,
    face_mass,
):
    wide_face = face_mass.shape[0]
    inner_width = hi_ainv.shape[0]
    geo_rows = hi_geom.shape[0]
    low_rows, low_particular = condense(
        lo_ainv,
        lo_geom,
        lo_load,
        lo_degree.astype(jnp.float32),
        lift_ref[:, :, :NF_LO, :NI_LO],
        trace_ref[:, :NI_LO, :, :NF_LO],
        face_mass[:NF_LO, :NF_LO],
    )
    record = jnp.concatenate(
        [hi_geom, hi_load.astype(jnp.float32), hi_degree.astype(jnp.float32)[None, :]], axis=0
    )
    outgoing = fill_buffer(record, hi_slot, hi_slot.shape[0])
    arrived = lax.all_to_all(outgoing, "deg", split_axis=1, concat_axis=1, tiled=True)
    high_rows, high_particular = condense(
        hi_ainv,
        arrived[:geo_rows],
        arrived[geo_rows : geo_rows + inner_width].astype(jnp.bfloat16),
        arrived[geo_rows + inner_width],
        lift_ref,
        trace_ref,
        face_mass,
    )
    groups = lax.axis_size("geo")
    cap_low = max(2, 6 * lo_ainv.shape[2] // groups)
    cap_high = max(2, 6 * hi_ainv.shape[2] // groups)
    per_owner = cap_low + cap_high
    face_total = (groups * per_owner + 1) // 2
    blocks = jnp.zeros((wide_face, wide_face, face_total), jnp.float32)
    right_side = jnp.zeros((wide_face, face_total), jnp.float32)
    low_positions = lo_send.reshape(-1)
    high_positions = hi_send.reshape(-1)
    low_target = jnp.where(
        low_positions < 0, -1, low_positions // cap_low * per_owner + low_positions % cap_low
    )
    high_target = jnp.where(
        high_positions < 0,
        -1,
        high_positions // cap_high * per_owner + cap_low + high_positions % cap_high,
    )
    combined = jnp.concatenate([embed_rows(low_rows, NF_LO, wide_face), high_rows], axis=1)
    positions = jnp.concatenate([low_target, high_target])
    arrived_rows = lax.all_to_all(
        fill_buffer(combined, positions, groups * per_owner),
        "geo",
        split_axis=1,
        concat_axis=1,
        tiled=True,
    )
    blocks, right_side = accumulate(blocks, right_side, arrived_rows, recv_face, wide_face)
    return (low_particular, high_particular, blocks, right_side)


def solution(mesh):
    in_specs = (
        P(None, None, ("geo", "deg")),
        P(None, ("geo", "deg")),
        P(None, ("geo", "deg")),
        P(("geo", "deg")),
        P(None, ("geo", "deg")),
        P(None, ("geo", "deg")),
        P(None, ("geo", "deg")),
        P(("geo", "deg")),
        P(("geo", "deg")),
        P(None, None, ("geo", "deg")),
        P(None, ("geo", "deg")),
        P(("geo", "deg")),
        P(),
        P(),
        P(),
    )
    out_specs = (
        P(None, ("geo", "deg")),
        P(None, ("geo", "deg")),
        P(None, None, ("geo", "deg")),
        P(None, ("geo", "deg")),
    )
    return jax.shard_map(
        on_device, mesh=mesh, in_specs=in_specs, out_specs=out_specs, check_vma=False
    )
```

profile of v0, /device:TPU:27, one launch (start us, length us, event | category | flops | bytes accessed | tf_op | source)
XLA Modules:
  0.0 220.3 jit_solution(9106446782423416625)
XLA Ops:
  0.6 0.7 convert_element_type.120
  1.4 0.7 convert_bitcast_fusion
  2.0 0.7 maximum_bitcast_fusion
  2.7 0.1 copy.105
  2.8 0.7 compare_select_fusion.2
  3.5 1.5 scatter_custom_fusion
  5.0 4.3 %all-to-all-start = ((f32[97,4,32]{0,2,1:T(8,128)}), f32[97,4,32]{0,2,1:T(8,128)S(1)}, u32[]{:S(2)}, u32[]{:S(2)}) async-start(f32[97,4,32]{0,2,1:T(8,128)} %bitcast.9), calls=%async_computation | async-start | bytes 131072 | tf_op jit(solution)/shard_map/all_to_all | solution.py:139
  9.2 0.7 broadcast_multiply_fusion.2
  9.9 0.7 bitcast_convert_fusion.2
  10.6 2.2 copy.112
  12.8 1.0 multiply_reduce_fusion.2
  13.7 0.6 bitcast_convert_fusion.1
  14.4 1.0 copy.113
  15.4 0.1 copy.108
  15.5 1.7 multiply_reduce_fusion.1
  17.2 1.7 copy.114
  18.9 0.9 slice.92
  19.8 0.2 copy.167
  20.1 1.2 fusion.35
  21.3 2.7 %copy.111 = bf16[20,4,10,128]{0,2,3,1:T(8,128)(2,1)} copy(bf16[20,4,10,128]{3,2,1,0:T(8,128)(2,1)S(1)} %fusion.35) | data formatting | bytes 409600 | tf_op jit(solution)/shard_map/convert_element_type | solution.py:39
  24.0 0.3 broadcast_multiply_fusion.1
  24.3 0.1 copy.107
  24.5 4.3 %fusion.7 = bf16[10,10,4,128]{0,1,3,2:T(8,128)(2,1)} fusion(bf16[4,10,20,128]{2,1,3,0:T(8,128)(2,1)S(1)} %copy.114, bf16[20,4,10,128]{0,2,3,1:T(8,128)(2,1)} %copy.111, f32[10,10,128]{0,1,2:T(8,128)S(1)} %broadcast_multiply_fusion.1, f32[4,128]{1,0:T(4,128)S(1)} %slice-done, f32[10,10]{0,1:T(8,128)S(1)} %copy.107, bf16[20,20,128]{1,0,2:T(8,128)(2,1)} %copy.112), kind=kOutput, calls=%fused_computation.14 | convolution fusion | flops 6451200 | bytes 668048 | tf_op jit(solution)/shard_map/aije,jame->imae/dot_general | solution.py:45
  28.8 0.6 compare_select_fusion
  29.4 0.1 copy.116
  29.5 3.7 %copy.124 = bf16[84,84,128]{1,0,2:T(8,128)(2,1)S(1)} copy(bf16[84,84,128]{2,1,0:T(8,128)(2,1)} %param.32) | data formatting | bytes 3612672 | tf_op args[9]
  33.2 2.8 %copy.115 = bf16[10,10,512]{2,1,0:T(8,128)(2,1)S(1)} copy(bf16[10,10,512]{0,1,2:T(8,128)(2,1)} %bitcast.161) | data formatting | bytes 204800 | tf_op jit(solution)/shard_map/reshape | solution.py:80
  36.0 1.0 pad.14
  37.0 2.2 reshape.456
  39.2 0.1 slice.103
  39.3 0.1 copy.166
  39.4 0.1 div.52
  39.5 0.1 fusion.47
  39.6 0.1 slice.128
  39.7 0.1 bitcast_multiply_fusion.2
  39.8 1.6 fusion.44
  41.4 0.1 bitcast_convert_fusion
  41.5 0.7 copy.170
  42.2 0.1 copy.122
  42.3 0.1 div.59
  42.4 0.1 copy.118
  42.5 0.1 fusion.73
  42.6 10.3 %multiply_reduce_fusion = (f32[128,4,28]{0,2,1:T(8,128)S(1)}, bf16[4,28,84,128]{3,2,1,0:T(8,128)(2,1)}) fusion(f32[128,84]{0,1:T(8,128)} %copy.170, f32[84,128]{1,0:T(8,128)S(1)} %copy.122, f32[28,128]{1,0:T(8,128)S(1)} %fusion.50, f32[4,128,1,1]{0,1,3,2:T(8,128)S(1)} %bitcast.173, f32[4,4,28,84]{3,1,2,0:T(4,128)S(1)} %copy-done.1), kind=kOutput, calls=%fused_computation.10 | convolution fusion | flops 65013760 | bytes 2718720 | tf_op jit(solution)/shard_map/kaij,ke->aije/dot_general | solution.py:27
  52.9 7.7 %copy.128 = bf16[4,28,84,128]{2,1,3,0:T(8,128)(2,1)} copy(bf16[4,28,84,128]{3,2,1,0:T(8,128)(2,1)} %get-tuple-element.74) | data formatting | bytes 4816896 | tf_op jit(solution)/shard_map/convert_element_type | solution.py:30
  60.6 9.3 %fusion.4 = bf16[84,4,28,128]{3,0,2,1:T(8,128)(2,1)} fusion(f32[28,128]{1,0:T(8,128)S(1)} %fusion.50, f32[84,128]{1,0:T(8,128)S(1)} %copy.122, f32[4,128,1,1]{0,1,3,2:T(8,128)S(1)} %bitcast.172, f32[4,84,4,28]{1,2,3,0:T(4,128)S(1)} %copy-done.3), kind=kOutput, calls=%fused_computation.9 | convolution fusion | flops 61415424 | bytes 2618368 | tf_op jit(solution)/shard_map/kjai,ke->jaie/dot_general | solution.py:33
  69.9 7.7 %copy.123 = bf16[84,4,28,128]{0,2,3,1:T(8,128)(2,1)} copy(bf16[84,4,28,128]{3,0,2,1:T(8,128)(2,1)} %fusion.4) | data formatting | bytes 4816896 | tf_op jit(solution)/shard_map/convert_element_type | solution.py:39
  77.6 1.9 broadcast_multiply_fusion
  79.5 0.1 copy.117
  79.6 8.0 %fusion = bf16[28,28,4,128]{0,1,3,2:T(8,128)(2,1)} fusion(f32[28,28,128]{0,1,2:T(8,128)} %broadcast_multiply_fusion, f32[4,128]{1,0:T(4,128)S(1)} %copy.117, f32[28,28]{0,1:T(8,128)S(1)} %copy.116, bf16[4,28,84,128]{2,1,3,0:T(8,128)(2,1)} %copy.128, bf16[84,4,28,128]{0,2,3,1:T(8,128)(2,1)} %copy.123, bf16[84,84,128]{1,0,2:T(8,128)(2,1)S(1)} %copy.124), kind=kOutput, calls=%fused_computation.3 | convolution fusion | flops 272556032 | bytes 7832640 | tf_op jit(solution)/shard_map/aije,jame->imae/dot_general | solution.py:45
  87.6 5.6 %copy.129 = bf16[28,28,4,128]{3,2,1,0:T(4,128)(2,1)S(1)} copy(bf16[28,28,4,128]{0,1,3,2:T(8,128)(2,1)} %fusion) | data formatting | bytes 1605632 | tf_op jit(solution)/shard_map/convert.4
  93.2 0.1 copy.190
  93.4 0.2 fusion.28
  93.7 2.4 %copy.130 = bf16[1024,812]{1,0:T(8,128)(2,1)} copy(bf16[1024,812]{0,1:T(8,128)(2,1)S(1)} %fusion.28) | data formatting | bytes 3325952 | tf_op jit(solution)/shard_map/concatenate | solution.py:166
  96.1 6.8 %scatter_custom_fusion.1 = bf16[812,1536]{0,1:T(8,128)(2,1)S(1)} fusion(s32[1024]{0:T(1024)} %bitcast.177, bf16[1024,812]{1,0:T(8,128)(2,1)} %copy.130, bf16[]{:T(256)} %constant.124.clone.1), kind=kCustom, calls=%fused_computation.37 | custom fusion | bytes 2494976 | tf_op jit(solution)/shard_map/scatter | solution.py:75
  102.9 2.6 %all_to_all.16 = bf16[812,128,12]{0,2,1:T(8,128)(2,1)} reshape(bf16[812,1536]{0,1:T(8,128)(2,1)S(1)} %scatter_custom_fusion.1) | data formatting | bytes 4988928 | tf_op jit(solution)/shard_map/all_to_all | solution.py:168
  105.5 18.6 %all-to-all-start.1 = ((bf16[812,128,12]{0,2,1:T(8,128)(2,1)}), bf16[812,128,12]{0,2,1:T(8,128)(2,1)}, u32[]{:S(2)}, u32[]{:S(2)}) async-start(bf16[812,128,12]{0,2,1:T(8,128)(2,1)} %all_to_all.16), calls=%async_computation.1 | async-start | bytes 7340032 | tf_op jit(solution)/shard_map/all_to_all | solution.py:168
  124.2 0.7 copy.131
  124.9 85.9 %all-to-all-done.1 = bf16[812,128,12]{0,2,1:T(8,128)(2,1)} async-done(((bf16[812,128,12]{0,2,1:T(8,128)(2,1)}), bf16[812,128,12]{0,2,1:T(8,128)(2,1)}, u32[]{:S(2)}, u32[]{:S(2)}) %all-to-all-start.1) | async-done | bytes 2494496 | tf_op jit(solution)/shard_map/all_to_all | solution.py:168
  210.8 4.3 %all_to_all.18 = bf16[812,1536]{0,1:T(8,128)(2,1)S(1)} reshape(bf16[812,128,12]{0,2,1:T(8,128)(2,1)} %all-to-all-done.1) | data formatting | bytes 4988928 | tf_op jit(solution)/shard_map/all_to_all | solution.py:168
  215.1 1.6 fusion.14
  216.7 1.2 fusion.30
  217.8 0.6 pad_maximum_fusion
  218.5 0.2 fusion.21
  218.7 1.7 add.188
  (35 shorter events, 0.2 us)
Async XLA Ops:
  0.6 19.4 %copy-start.4 = (f32[12,128]{1,0:T(8,128)S(1)}, f32[12,128]{1,0:T(8,128)}, u32[]{:S(2)}) copy-start(f32[12,128]{1,0:T(8,128)} %param.24) | copy-start | bytes 18436
  5.0 34.3 %all-to-all-start = ((f32[97,4,32]{0,2,1:T(8,128)}), f32[97,4,32]{0,2,1:T(8,128)S(1)}, u32[]{:S(2)}, u32[]{:S(2)}) async-start(f32[97,4,32]{0,2,1:T(8,128)} %bitcast.9), calls=%async_computation | async-start | bytes 131072 | tf_op jit(solution)/shard_map/all_to_all | solution.py:139
  18.9 5.5 %copy-start.2 = (f32[28,28]{1,0:T(8,128)S(1)}, f32[28,28]{1,0:T(8,128)}, u32[]{:S(2)}) copy-start(f32[28,28]{1,0:T(8,128)} %param.37) | copy-start | bytes 9412
  18.9 5.6 %copy-start.5 = (s32[4,128]{1,0:T(4,128)S(1)}, s32[4,128]{1,0:T(4,128)}, u32[]{:S(2)}) copy-start(s32[4,128]{1,0:T(4,128)} %param.27) | copy-start | bytes 6148
  18.9 5.6 %copy-start.6 = (s32[4,128]{1,0:T(4,128)S(1)}, s32[4,128]{1,0:T(4,128)}, u32[]{:S(2)}) copy-start(s32[4,128]{1,0:T(4,128)} %param.33) | copy-start | bytes 6148
  18.9 5.6 %slice-start = ((f32[12,128]{1,0:T(8,128)}), f32[4,128]{1,0:T(4,128)S(1)}, s32[]{:S(2)}) async-start(f32[12,128]{1,0:T(8,128)} %param.24), calls=%async_computation.2 | async-start | bytes 4096 | tf_op jit(solution)/shard_map/slice | solution.py:46
  37.0 5.6 %copy-start.1 = (f32[4,4,28,84]{3,1,2,0:T(4,128)S(1)}, f32[4,4,28,84]{3,1,2,0:T(4,128)}, u32[]{:S(2)}) copy-start(f32[4,4,28,84]{3,1,2,0:T(4,128)} %param.35) | copy-start | bytes 451588
  52.9 7.7 %copy-start.3 = (f32[4,84,4,28]{1,2,3,0:T(4,128)S(1)}, f32[4,84,4,28]{1,2,3,0:T(4,128)}, u32[]{:S(2)}) copy-start(f32[4,84,4,28]{1,2,3,0:T(4,128)} %param.36) | copy-start | bytes 451588
  87.6 5.8 %copy-start = (bf16[784,512]{1,0:T(8,128)(2,1)S(1)}, bf16[784,512]{1,0:T(8,128)(2,1)}, u32[]{:S(2)}) copy-start(bf16[784,512]{1,0:T(8,128)(2,1)} %reshape.456) | copy-start | bytes 2408452
  105.5 105.3 %all-to-all-start.1 = ((bf16[812,128,12]{0,2,1:T(8,128)(2,1)}), bf16[812,128,12]{0,2,1:T(8,128)(2,1)}, u32[]{:S(2)}, u32[]{:S(2)}) async-start(bf16[812,128,12]{0,2,1:T(8,128)(2,1)} %all_to_all.16), calls=%async_computation.1 | async-start | bytes 7340032 | tf_op jit(solution)/shard_map/all_to_all | solution.py:168
  124.9 90.2 %copy-start.7 = (s32[1536]{0:T(1024)S(1)}, s32[1536]{0:T(1024)}, u32[]{:S(2)}) copy-start(s32[1536]{0:T(1024)} %param.34) | copy-start | bytes 18436
where the time goes:
time: 222 us; the launch traced here: 220 us
  waiting for transfers between devices  85.9 us (39%)
  local copies, waits for them, and re-layouts  61.4 us (28%)
  matrix products  39.2 us (18%)
  starting transfers between devices  22.9 us (10%)
  other arithmetic  9.99 us (4%)
    all_to_all x1, waiting for transfers between devices, on_device(): lax.all_to_all(fill_buffer(combined, positions, groups * per_owner), 'geo...  85.9 us
    all_to_all x1, starting transfers between devices, on_device(): lax.all_to_all(fill_buffer(combined, positions, groups * per_owner), 'geo...  18.6 us
    dot_general x2, matrix products, condense(): jnp.einsum('aije,jame->imae', lift_mat, solved, preferred_element_type=jn...  12.3 us
    dot_general x2, matrix products, condense(): jnp.einsum('kaij,ke->aije', lift_table, geometry[:term_count], precision=...  12 us
    dot_general x2, matrix products, condense(): jnp.einsum('kjai,ke->jaie', trace_table, geometry[term_count:2 * term_cou...  10.5 us
    convert_element_type x2, local copies, waits for them, and re-layouts, condense(): (trace_mix * inner_mask[:, None, None, :] * face_mask[None, None, :, :])....  10.4 us
    convert_element_type x2, local copies, waits for them, and re-layouts, condense(): (lift_mix * face_mask[None, :, None, :] * inner_mask[None, None, :, :]).a...  9.37 us
    unnamed x31, local copies, waits for them, and re-layouts  8.98 us
  transfers between devices with their start and end apart: 2, of which 1 were waited for; matrix products, arithmetic and copies ran while one was open for 14% of the time, Pallas kernels for 0%

commit v1 on v0

--- a/solution.py
+++ b/solution.py
@@ -1,3 +1,4 @@
+import functools
 import jax
 import jax.numpy as jnp
 from jax import lax
@@ -5,6 +6,22 @@
 
 NI_LO = 20
 NF_LO = 10
+
+
+def check_tasks(own_rows, along_axis, d_out, d0):
+    big = jnp.concatenate(
+        jax.lax.all_to_all(
+            jnp.stack(jnp.split(own_rows, jax.lax.axis_size(along_axis), axis=d_out)),
+            axis_name=along_axis,
+            split_axis=0,
+            concat_axis=0,
+        ),
+        axis=d0,
+    )
+    return big
+
+
+drive_orders_now = functools.partial(check_tasks, along_axis="geo", d_out=1, d0=1)
 
 
 def prefix_masks(degree_value, inner_width, face_width):
@@ -165,13 +182,7 @@
     )
     combined = jnp.concatenate([embed_rows(low_rows, NF_LO, wide_face), high_rows], axis=1)
     positions = jnp.concatenate([low_target, high_target])
-    arrived_rows = lax.all_to_all(
-        fill_buffer(combined, positions, groups * per_owner),
-        "geo",
-        split_axis=1,
-        concat_axis=1,
-        tiled=True,
-    )
+    arrived_rows = drive_orders_now(fill_buffer(combined, positions, groups * per_owner))
     blocks, right_side = accumulate(blocks, right_side, arrived_rows, recv_face, wide_face)
     return (low_particular, high_particular, blocks, right_side)
 

time: 222 us -> 297 us (1.34)
  local copies, waits for them, and re-layouts: 61.4 us -> 137 us
    unnamed x31 -> x158, local copies, waits for them, and re-layouts: 8.98 us -> 86.8 us
    all_to_all x2 -> x0, local copies, waits for them, and re-layouts: 6.91 us -> none  [on_device(): lax.all_to_all(fill_buffer(combined, positions, groups * per_owner), 'geo...]
    reshape x0 -> x1, local copies, waits for them, and re-layouts: none -> 4.28 us  [check_tasks(): jnp.concatenate(jax.lax.all_to_all(jnp.stack(jnp.split(own_rows, jax.lax....]
    another operation x1 -> x2, local copies, waits for them, and re-layouts: 5.57 us -> 6.18 us
  transfers between devices with their start and end apart: 2 -> 2, of which waited for: 1 -> 1; matrix products, arithmetic and copies ran while one was open for 14% -> 10% of each run, Pallas kernels for 0% -> 0%
where the time goes in v1:
time: 297 us; the launch traced here: 296 us
  local copies, waits for them, and re-layouts  137 us (46%)
  waiting for transfers between devices  85.9 us (29%)
  matrix products  39.2 us (13%)
  starting transfers between devices  22.9 us (8%)
  other arithmetic  9.99 us (3%)
    unnamed x158, local copies, waits for them, and re-layouts  86.8 us
    all_to_all x1, waiting for transfers between devices, check_tasks(): jax.lax.all_to_all(jnp.stack(jnp.split(own_rows, jax.lax.axis_size(along_...  85.9 us
    all_to_all x1, starting transfers between devices, check_tasks(): jax.lax.all_to_all(jnp.stack(jnp.split(own_rows, jax.lax.axis_size(along_...  18.6 us
    dot_general x2, matrix products, condense(): jnp.einsum('aije,jame->imae', lift_mat, solved, preferred_element_type=jn...  12.3 us
    dot_general x2, matrix products, condense(): jnp.einsum('kaij,ke->aije', lift_table, geometry[:term_count], precision=...  12 us
    dot_general x2, matrix products, condense(): jnp.einsum('kjai,ke->jaie', trace_table, geometry[term_count:2 * term_cou...  10.5 us
    convert_element_type x2, local copies, waits for them, and re-layouts, condense(): (trace_mix * inner_mask[:, None, None, :] * face_mask[None, None, :, :])....  10.4 us
    convert_element_type x2, local copies, waits for them, and re-layouts, condense(): (lift_mix * face_mask[None, :, None, :] * inner_mask[None, None, :, :]).a...  9.37 us
  transfers between devices with their start and end apart: 2, of which 1 were waited for; matrix products, arithmetic and copies ran while one was open for 10% of the time, Pallas kernels for 0%

profile of v1, /device:TPU:27, one launch (start us, length us, event | category | flops | bytes accessed | tf_op | source)
XLA Modules:
  0.0 296.1 jit_solution(16014224589356669075)
XLA Ops:
  0.6 0.7 convert_element_type.120
  1.4 0.7 convert_bitcast_fusion
  2.0 0.7 maximum_bitcast_fusion
  2.8 0.7 compare_select_fusion.2
  3.5 1.5 scatter_custom_fusion
  5.0 4.3 %all-to-all-start = ((f32[97,4,32]{0,2,1:T(8,128)}), f32[97,4,32]{0,2,1:T(8,128)S(1)}, u32[]{:S(2)}, u32[]{:S(2)}) async-start(f32[97,4,32]{0,2,1:T(8,128)} %bitcast.9), calls=%async_computation | async-start | bytes 131072 | tf_op jit(solution)/shard_map/all_to_all | solution.py:156
  9.2 0.7 broadcast_multiply_fusion.2
  9.9 0.7 bitcast_convert_fusion.2
  10.6 2.2 copy.112
  12.8 1.0 multiply_reduce_fusion.2
  14.4 1.0 copy.113
  15.5 1.7 multiply_reduce_fusion.1
  17.2 1.7 copy.114
  18.9 0.9 slice.92
  20.0 1.2 fusion.35
  21.3 2.7 copy.111
  24.5 4.3 %fusion.7 = bf16[10,10,4,128]{0,1,3,2:T(8,128)(2,1)} fusion(bf16[4,10,20,128]{2,1,3,0:T(8,128)(2,1)S(1)} %copy.114, bf16[20,4,10,128]{0,2,3,1:T(8,128)(2,1)} %copy.111, f32[10,10,128]{0,1,2:T(8,128)S(1)} %broadcast_multiply_fusion.1, f32[4,128]{1,0:T(4,128)S(1)} %slice-done, f32[10,10]{0,1:T(8,128)S(1)} %copy.107, bf16[20,20,128]{1,0,2:T(8,128)(2,1)} %copy.112), kind=kOutput, calls=%fused_computation.14 | convolution fusion | flops 6451200 | bytes 668048 | tf_op jit(solution)/shard_map/aije,jame->imae/dot_general | solution.py:62
  29.5 3.7 %copy.124 = bf16[84,84,128]{1,0,2:T(8,128)(2,1)S(1)} copy(bf16[84,84,128]{2,1,0:T(8,128)(2,1)} %param.32) | data formatting | bytes 3612672 | tf_op args[9]
  33.2 2.8 copy.115
  36.0 1.0 pad.14
  37.0 2.1 reshape.460
  39.7 1.6 fusion.44
  41.4 0.7 copy.170
  42.6 10.3 %multiply_reduce_fusion = (f32[128,4,28]{0,2,1:T(8,128)S(1)}, bf16[4,28,84,128]{3,2,1,0:T(8,128)(2,1)}) fusion(f32[128,84]{0,1:T(8,128)} %copy.170, f32[84,128]{1,0:T(8,128)S(1)} %copy.122, f32[28,128]{1,0:T(8,128)S(1)} %fusion.50, f32[4,128,1,1]{0,1,3,2:T(8,128)S(1)} %bitcast.684, f32[4,4,28,84]{3,1,2,0:T(4,128)S(1)} %copy-done.1), kind=kOutput, calls=%fused_computation.10 | convolution fusion | flops 65013760 | bytes 2718720 | tf_op jit(solution)/shard_map/kaij,ke->aije/dot_general | solution.py:44
  52.9 7.7 %copy.128 = bf16[4,28,84,128]{2,1,3,0:T(8,128)(2,1)} copy(bf16[4,28,84,128]{3,2,1,0:T(8,128)(2,1)} %get-tuple-element.74) | data formatting | bytes 4816896 | tf_op jit(solution)/shard_map/convert_element_type | solution.py:47
  60.6 9.3 %fusion.4 = bf16[84,4,28,128]{3,0,2,1:T(8,128)(2,1)} fusion(f32[28,128]{1,0:T(8,128)S(1)} %fusion.50, f32[84,128]{1,0:T(8,128)S(1)} %copy.122, f32[4,128,1,1]{0,1,3,2:T(8,128)S(1)} %bitcast.683, f32[4,84,4,28]{1,2,3,0:T(4,128)S(1)} %copy-done.3), kind=kOutput, calls=%fused_computation.9 | convolution fusion | flops 61415424 | bytes 2618368 | tf_op jit(solution)/shard_map/kjai,ke->jaie/dot_general | solution.py:50
  69.9 7.7 %copy.123 = bf16[84,4,28,128]{0,2,3,1:T(8,128)(2,1)} copy(bf16[84,4,28,128]{3,0,2,1:T(8,128)(2,1)} %fusion.4) | data formatting | bytes 4816896 | tf_op jit(solution)/shard_map/convert_element_type | solution.py:56
  77.6 1.9 broadcast_multiply_fusion
  79.6 8.0 %fusion = bf16[28,28,4,128]{0,1,3,2:T(8,128)(2,1)} fusion(f32[28,28,128]{0,1,2:T(8,128)} %broadcast_multiply_fusion, f32[4,128]{1,0:T(4,128)S(1)} %copy.117, f32[28,28]{0,1:T(8,128)S(1)} %copy.116, bf16[4,28,84,128]{2,1,3,0:T(8,128)(2,1)} %copy.128, bf16[84,4,28,128]{0,2,3,1:T(8,128)(2,1)} %copy.123, bf16[84,84,128]{1,0,2:T(8,128)(2,1)S(1)} %copy.124), kind=kOutput, calls=%fused_computation.3 | convolution fusion | flops 272556032 | bytes 7832640 | tf_op jit(solution)/shard_map/aije,jame->imae/dot_general | solution.py:62
  87.6 5.6 %copy.129 = bf16[28,28,4,128]{3,2,1,0:T(4,128)(2,1)S(1)} copy(bf16[28,28,4,128]{0,1,3,2:T(8,128)(2,1)} %fusion) | data formatting | bytes 1605632 | tf_op jit(solution)/shard_map/convert.4
  93.6 2.4 copy.130
  96.1 6.8 %scatter_custom_fusion.1 = bf16[812,1536]{0,1:T(8,128)(2,1)S(1)} fusion(s32[1024]{0:T(1024)} %bitcast.688, bf16[1024,812]{1,0:T(8,128)(2,1)} %copy.130, bf16[]{:T(256)} %constant.124.clone.1), kind=kCustom, calls=%fused_computation.37 | custom fusion | bytes 2494976 | tf_op jit(solution)/shard_map/scatter | solution.py:92
  108.3 0.6 constant_dynamic-update-slice_fusion.118
  111.4 0.6 constant_dynamic-update-slice_fusion.113
  113.3 0.6 constant_dynamic-update-slice_fusion.110
  118.1 0.6 constant_dynamic-update-slice_fusion.102
  123.0 0.6 constant_dynamic-update-slice_fusion.94
  126.7 0.6 constant_dynamic-update-slice_fusion.88
  127.3 0.6 constant_dynamic-update-slice_fusion.87
  127.9 0.6 constant_dynamic-update-slice_fusion.86
  131.6 0.6 constant_dynamic-update-slice_fusion.80
  132.8 0.6 constant_dynamic-update-slice_fusion.78
  136.5 0.6 constant_dynamic-update-slice_fusion.72
  137.8 0.6 constant_dynamic-update-slice_fusion.70
  140.2 0.6 constant_dynamic-update-slice_fusion.66
  141.4 0.6 constant_dynamic-update-slice_fusion.64
  142.7 0.6 constant_dynamic-update-slice_fusion.62
  145.2 0.6 constant_dynamic-update-slice_fusion.58
  146.4 0.6 constant_dynamic-update-slice_fusion.56
  151.3 0.6 constant_dynamic-update-slice_fusion.48
  152.5 0.6 constant_dynamic-update-slice_fusion.46
  156.2 0.6 constant_dynamic-update-slice_fusion.40
  166.0 0.6 constant_dynamic-update-slice_fusion.24
  170.9 0.6 constant_dynamic-update-slice_fusion.16
  174.6 0.6 constant_dynamic-update-slice_fusion.10
  177.0 0.6 constant_dynamic-update-slice_fusion.6
  181.3 18.6 %all-to-all-start.1 = ((bf16[128,812,12]{1,2,0:T(8,128)(2,1)}), bf16[128,812,12]{1,2,0:T(8,128)(2,1)}, u32[]{:S(2)}, u32[]{:S(2)}) async-start(bf16[128,812,12]{1,2,0:T(8,128)(2,1)} %constant_dynamic-update-slice_fusion), calls=%async_computation.1 | async-start | bytes 7340032 | tf_op jit(solution)/shard_map/all_to_all | solution.py:13
  200.0 0.7 copy.131
  200.7 85.9 %all-to-all-done.1 = bf16[128,812,12]{1,2,0:T(8,128)(2,1)} async-done(((bf16[128,812,12]{1,2,0:T(8,128)(2,1)}), bf16[128,812,12]{1,2,0:T(8,128)(2,1)}, u32[]{:S(2)}, u32[]{:S(2)}) %all-to-all-start.1) | async-done | bytes 2494496 | tf_op jit(solution)/shard_map/all_to_all | solution.py:13
  286.6 4.3 %reshape.465 = bf16[812,1536]{0,1:T(8,128)(2,1)S(1)} reshape(bf16[812,128,12]{0,2,1:T(8,128)(2,1)} %bitcast.175) | data formatting | bytes 4988928 | tf_op jit(solution)/shard_map/reshape | solution.py:12
  290.9 1.6 fusion.14
  292.5 1.2 fusion.30
  293.7 0.6 pad_maximum_fusion
  294.5 1.7 add.188
  (162 shorter events, 67.4 us)
Async XLA Ops:
  0.6 19.4 %copy-start.4 = (f32[12,128]{1,0:T(8,128)S(1)}, f32[12,128]{1,0:T(8,128)}, u32[]{:S(2)}) copy-start(f32[12,128]{1,0:T(8,128)} %param.24) | copy-start | bytes 18436
  5.0 34.2 %all-to-all-start = ((f32[97,4,32]{0,2,1:T(8,128)}), f32[97,4,32]{0,2,1:T(8,128)S(1)}, u32[]{:S(2)}, u32[]{:S(2)}) async-start(f32[97,4,32]{0,2,1:T(8,128)} %bitcast.9), calls=%async_computation | async-start | bytes 131072 | tf_op jit(solution)/shard_map/all_to_all | solution.py:156
  15.5 8.8 %copy-start.2 = (f32[28,28]{1,0:T(8,128)S(1)}, f32[28,28]{1,0:T(8,128)}, u32[]{:S(2)}) copy-start(f32[28,28]{1,0:T(8,128)} %param.37) | copy-start | bytes 9412
  17.2 7.2 %copy-start.5 = (s32[4,128]{1,0:T(4,128)S(1)}, s32[4,128]{1,0:T(4,128)}, u32[]{:S(2)}) copy-start(s32[4,128]{1,0:T(4,128)} %param.27) | copy-start | bytes 6148
  17.2 7.3 %copy-start.6 = (s32[4,128]{1,0:T(4,128)S(1)}, s32[4,128]{1,0:T(4,128)}, u32[]{:S(2)}) copy-start(s32[4,128]{1,0:T(4,128)} %param.33) | copy-start | bytes 6148
  17.2 7.3 %slice-start = ((f32[12,128]{1,0:T(8,128)}), f32[4,128]{1,0:T(4,128)S(1)}, s32[]{:S(2)}) async-start(f32[12,128]{1,0:T(8,128)} %param.24), calls=%async_computation.2 | async-start | bytes 4096 | tf_op jit(solution)/shard_map/slice | solution.py:63
  36.0 6.6 %copy-start.1 = (f32[4,4,28,84]{3,1,2,0:T(4,128)S(1)}, f32[4,4,28,84]{3,1,2,0:T(4,128)}, u32[]{:S(2)}) copy-start(f32[4,4,28,84]{3,1,2,0:T(4,128)} %param.35) | copy-start | bytes 451588
  52.9 7.7 %copy-start.3 = (f32[4,84,4,28]{1,2,3,0:T(4,128)S(1)}, f32[4,84,4,28]{1,2,3,0:T(4,128)}, u32[]{:S(2)}) copy-start(f32[4,84,4,28]{1,2,3,0:T(4,128)} %param.36) | copy-start | bytes 451588
  87.6 5.8 %copy-start = (bf16[784,512]{1,0:T(8,128)(2,1)S(1)}, bf16[784,512]{1,0:T(8,128)(2,1)}, u32[]{:S(2)}) copy-start(bf16[784,512]{1,0:T(8,128)(2,1)} %reshape.460) | copy-start | bytes 2408452
  181.3 105.3 %all-to-all-start.1 = ((bf16[128,812,12]{1,2,0:T(8,128)(2,1)}), bf16[128,812,12]{1,2,0:T(8,128)(2,1)}, u32[]{:S(2)}, u32[]{:S(2)}) async-start(bf16[128,812,12]{1,2,0:T(8,128)(2,1)} %constant_dynamic-update-slice_fusion), calls=%async_computation.1 | async-start | bytes 7340032 | tf_op jit(solution)/shard_map/all_to_all | solution.py:13
  200.0 90.9 %copy-start.7 = (s32[1536]{0:T(1024)S(1)}, s32[1536]{0:T(1024)}, u32[]{:S(2)}) copy-start(s32[1536]{0:T(1024)} %param.34) | copy-start | bytes 18436
